TPU v7x, 32 devices: a whole 2x2x4 slice. The times are simulated.
32 devices in a mesh: mem: 4 (over z), lat: 8 (over y, x, core).
Axes of the slice: x: 2, y: 2, z: 4, core: 2. Of those that a mesh axis runs over, the one named last changes fastest.
Arguments:
- features: bfloat16 [16, 16, 1440, 128], P('mem', 'lat'), may hold values from -6 to 6
- conv_inner: bfloat16 [3, 3, 128, 128], replicated, may hold values from -0.1875 to 0.1875
- conv_head: bfloat16 [3, 3, 128, 69], replicated, may hold values from -0.1875 to 0.1875
- truth: float32 [69, 16, 1440], P(None, 'lat'), may hold values from -5 to 5
- kernel_width: float32 [69], replicated, may hold values from 0.3 to 1.5
- var_weight: float32 [69], replicated, may hold values from 0.5 to 2
Outputs:
- grad_features: bfloat16 [16, 16, 1440, 128], P('mem', 'lat')
- grad_inner: float32 [3, 3, 128, 128], replicated
- grad_head: float32 [3, 3, 128, 69], replicated
All inputs are finite; a program needn't handle non-finite values.
Results may differ from a plain program's by a relative error of at most 0.0098.
Values may be sent and summed in bfloat16 or wider, within the bound.
No kernel may reach another device: no remote copies, remote signals or barrier semaphores. Data moves between devices by JAX's collectives and lax.ppermute only.
A program may use at most 256 MiB of HBM per device.

v0:
```python
import jax
import jax.numpy as jnp
from jax import lax
from jax.sharding import PartitionSpec as P


def padded_2(cells, sides, width):
    for axis, dim in sides:
        count = lax.axis_size(axis)
        ends = count - 1
        head = lax.slice_in_dim(cells, 0, width, axis=dim)
        tail = lax.slice_in_dim(cells, cells.shape[dim] - width, cells.shape[dim], axis=dim)
        cells = jnp.concatenate(
            [
                lax.ppermute(tail, axis, [(i, (i + 1) % count) for i in range(ends)]),
                cells,
                lax.ppermute(head, axis, [((i + 1) % count, i) for i in range(ends)]),
            ],
            axis=dim,
        )
    return cells


def wrap_lon(values, axis):
    count = values.shape[axis]
    return jnp.concatenate(
        [
            lax.slice_in_dim(values, count - 1, count, axis=axis),
            values,
            lax.slice_in_dim(values, 0, 1, axis=axis),
        ],
        axis=axis,
    )


def gelu_slope(pre):
    return jax.jvp(jax.nn.gelu, (pre,), (jnp.ones_like(pre),))[1]


def hidden_conv(padded, kernel, band_rows):
    lon_cells = padded.shape[2] - 2
    summed = jnp.zeros((padded.shape[0], band_rows, lon_cells, kernel.shape[3]), jnp.float32)
    for row_off in range(3):
        for col_off in range(3):
            summed = summed + jnp.einsum(
                "mrlc,co->mrlo",
                padded[:, row_off : row_off + band_rows, col_off : col_off + lon_cells],
                kernel[row_off, col_off],
                preferred_element_type=jnp.float32,
            )
    return summed


def field_conv(padded, kernel, band_rows):
    lon_cells = padded.shape[2] - 2
    summed = jnp.zeros((padded.shape[0], kernel.shape[3], band_rows, lon_cells), jnp.float32)
    for row_off in range(3):
        for col_off in range(3):
            summed = summed + jnp.einsum(
                "mrlc,cv->mvrl",
                padded[:, row_off : row_off + band_rows, col_off : col_off + lon_cells],
                kernel[row_off, col_off],
                preferred_element_type=jnp.float32,
            )
    return summed


def field_back(padded_grad, kernel, band_rows):
    lon_cells = padded_grad.shape[3] - 2
    summed = jnp.zeros((padded_grad.shape[0], band_rows, lon_cells, kernel.shape[2]), jnp.float32)
    for row_off in range(3):
        for col_off in range(3):
            summed = summed + jnp.einsum(
                "mvrl,cv->mrlc",
                padded_grad[
                    :,
                    :,
                    2 - row_off : 2 - row_off + band_rows,
                    2 - col_off : 2 - col_off + lon_cells,
                ],
                kernel[row_off, col_off],
                preferred_element_type=jnp.float32,
            )
    return summed


def hidden_back(padded_grad, kernel, band_rows):
    lon_cells = padded_grad.shape[2] - 2
    summed = jnp.zeros((padded_grad.shape[0], band_rows, lon_cells, kernel.shape[2]), jnp.float32)
    for row_off in range(3):
        for col_off in range(3):
            summed = summed + jnp.einsum(
                "mrlo,co->mrlc",
                padded_grad[
                    :, 2 - row_off : 2 - row_off + band_rows, 2 - col_off : 2 - col_off + lon_cells
                ],
                kernel[row_off, col_off],
                preferred_element_type=jnp.float32,
            )
    return summed


def kernel_grad(padded_input, grad_out, form, band_rows, lon_cells):
    pieces = []
    for row_off in range(3):
        for col_off in range(3):
            pieces.append(
                jnp.einsum(
                    form,
                    padded_input[:, row_off : row_off + band_rows, col_off : col_off + lon_cells],
                    grad_out,
                    preferred_element_type=jnp.float32,
                )
            )
    return jnp.stack(pieces).reshape((3, 3) + pieces[0].shape)


def pair_sums(own, others, inverse):
    spread = others[None] - own[:, None]
    kernel = jnp.exp(-0.5 * spread * spread * inverse[None, None, :, None, None])
    return jnp.sum(kernel * spread, axis=1)


def member_grad(own, pairwise, truth_piece, inverse, var_weight, members):
    offset = own - truth_piece[None]
    nearness = jnp.exp(-0.5 * offset * offset * inverse[None, :, None, None])
    scale = (var_weight * inverse)[None, :, None, None]
    return scale * (2.0 / (members - 1) * pairwise + 2.0 * nearness * offset)


def split_groups(values, blocks, group):
    shaped = values.reshape((values.shape[0], blocks, group) + values.shape[2:])
    return jnp.moveaxis(shaped, 1, 0)


def shards(features, conv_inner, conv_head, truth, kernel_width, var_weight):
    band_rows = features.shape[1]
    lon_cells = features.shape[2]
    variables = conv_head.shape[3]
    feature_ext = padded_2(features, (("lat", 1),), 1)
    pre_own = hidden_conv(wrap_lon(feature_ext, 2), conv_inner, band_rows)
    hidden_own = jax.nn.gelu(pre_own).astype(jnp.bfloat16)
    hidden_ext = padded_2(hidden_own, (("lat", 1),), 1)
    hidden_wrap = wrap_lon(hidden_ext, 2)
    field = field_conv(hidden_wrap, conv_head, band_rows).astype(jnp.bfloat16)
    inverse = 1.0 / (kernel_width * kernel_width)
    group = 3
    blocks = variables // group
    inverse_blocks = inverse.reshape(blocks, group)
    gathered = lax.all_to_all(field, "mem", split_axis=3, concat_axis=0, tiled=True)
    values = gathered.astype(jnp.float32)
    members = values.shape[0]
    piece_cells = values.shape[3]

    def block_pairs(packed):
        member_values, rates = packed
        return pair_sums(member_values, member_values, rates)

    pairwise = lax.map(block_pairs, (split_groups(values, blocks, group), inverse_blocks))
    pairwise = jnp.moveaxis(pairwise, 0, 1).reshape(values.shape)
    truth_piece = lax.dynamic_slice_in_dim(
        truth, lax.axis_index("mem") * piece_cells, piece_cells, 2
    )
    gradient = member_grad(values, pairwise, truth_piece, inverse, var_weight, members).astype(
        jnp.bfloat16
    )
    field_grad = lax.all_to_all(gradient, "mem", split_axis=0, concat_axis=3, tiled=True)
    grad_pad = padded_2(field_grad, (("lat", 2),), 1)
    hidden_grad = (
        field_back(wrap_lon(grad_pad, 3), conv_head, band_rows) * gelu_slope(pre_own)
    ).astype(jnp.bfloat16)
    head_grad = kernel_grad(hidden_wrap, field_grad, "mrlc,mvrl->cv", band_rows, lon_cells)
    hidden_pad = padded_2(hidden_grad, (("lat", 1),), 1)
    grad_features = hidden_back(wrap_lon(hidden_pad, 2), conv_inner, band_rows).astype(jnp.bfloat16)
    inner_grad = kernel_grad(
        wrap_lon(feature_ext, 2), hidden_grad, "mrlc,mrlo->co", band_rows, lon_cells
    )
    inner_sum, head_sum = lax.psum((inner_grad, head_grad), ("mem", "lat"))
    points = band_rows * lax.axis_size("lat") * lon_cells
    return (grad_features, inner_sum / points, head_sum / points)


def solution(mesh):
    in_specs = (P("mem", "lat", None, None), P(), P(), P(None, "lat", None), P(), P())
    out_specs = (P("mem", "lat", None, None), P(), P())
    return jax.shard_map(shards, mesh=mesh, in_specs=in_specs, out_specs=out_specs, check_vma=False)
```

profile of v0, /device:TPU:0, one launch (start us, length us, event | category | flops | bytes accessed | tf_op | source)
XLA Modules:
  0.0 686.2 jit_solution(3638382335253527599)
XLA Ops:
  19.7 4.1 fusion.183
  23.7 4.0 fusion.173
  44.7 21.2 %multiply_convert_fusion = (bf16[4,2,1440,128]{3,2,1,0:T(8,128)(2,1)}, f32[4,2,1440,128]{3,2,1,0:T(8,128)}) fusion(bf16[3,3,128,128]{3,2,1,0:T(8,128)(2,1)S(1)} %copy-done.21, bf16[4,4,1,128]{3,2,1,0:T(2,128)(2,1)S(1)} %get-tuple-element.58, bf16[4,4,1440,128]{3,2,1,0:T(8,128)(2,1)} %copy-done.2, f32[4,2,1440,128]{3,2,1,0:T(8,128)} %fusion.168, ...), kind=kOutput, calls=%fused_computation.41 | convolution fusion | flops 408453120 | bytes 61972480 | tf_op jit(solution)/shard_map/mrlc,co->mrlo/dot_general | solution.py:45
  68.1 30.4 %collective-permute-start.2 = (bf16[4,1,1440,128]{3,2,1,0:T(8,128)(2,1)S(1)}, bf16[4,1,1440,128]{3,2,1,0:T(8,128)(2,1)S(1)}, u32[]{:S(2)}, u32[]{:S(2)}) collective-permute-start(bf16[4,1,1440,128]{3,2,1,0:T(8,128)(2,1)S(1)} %get-tuple-element.64), channel_id=1, source_target_pairs={{0,1},{1,2},{2,3},{3,4},{4,5},{5,6},{6,7},{8,9},{9,10},{10,11},{11... | collective-permute-start | bytes 4423688 | tf_op jit(solution)/shard_map/ppermute | solution.py:15
  103.7 7.3 %fusion.7 = (bf16[4,4,1441,128]{3,2,1,0:T(8,128)(2,1)S(1)}, bf16[4,4,1441,128]{3,2,1,0:T(8,128)(2,1)S(1)}) fusion(bf16[4,1,1440,128]{3,2,1,0:T(8,128)(2,1)S(1)} %collective-permute-done.3, bf16[4,2,1440,128]{3,2,1,0:T(8,128)(2,1)S(1)} %copy-done.5, bf16[4,1,1440,128]{3,2,1,0:T(8,128)(2,1)S(1)} %collective-permute-done.2), kind=kLoop, calls=%fused_computation.26 | loop fusion | flops 70828032 | bytes 17702912 | tf_op jit(solution)/shard_map/concatenate | solution.py:26
  111.0 4.1 fusion.76
  133.2 8.2 %fusion.71 = bf16[4,69,2,1440]{3,1,2,0:T(8,128)(2,1)} fusion(bf16[4,4,1441,128]{3,2,1,0:T(8,128)(2,1)S(1)} %get-tuple-element.57, f32[4,2,1440,69]{2,3,1,0:T(8,128)S(1)} %fusion.53, f32[4,2,1440,69]{2,3,1,0:T(8,128)} %fusion.76, f32[4,2,1440,69]{2,3,1,0:T(8,128)} %fusion.80, f32[4,2,1440,69]{2,3,1,0:T(8,128)S(1)} %fusion.218, ...), kind=kOutput, calls=%fused_computation.109 | convolution fusion | flops 210643200 | bytes 32868864 | tf_op jit(solution)/shard_map/mrlc,cv->mvrl/dot_general | solution.py:59
  141.4 8.4 %copy.54 = bf16[4,69,2,1440]{1,2,0,3:T(2,128)(2,1)} copy(bf16[4,69,2,1440]{3,1,2,0:T(8,128)(2,1)} %fusion.71) | data formatting | bytes 3179520 | tf_op jit(solution)/shard_map/convert_element_type | solution.py:145
  149.8 4.9 all-to-all-start
  155.2 46.0 %all-to-all-done = bf16[4,69,2,1440]{1,2,0,3:T(2,128)(2,1)} async-done(((bf16[4,69,2,1440]{1,2,0,3:T(2,128)(2,1)}), bf16[4,69,2,1440]{1,2,0,3:T(2,128)(2,1)}, u32[]{:S(2)}, u32[]{:S(2)}) %all-to-all-start) | async-done | bytes 1589792 | tf_op jit(solution)/shard_map/all_to_all | solution.py:150
  201.1 7.7 %copy.55 = bf16[4,69,2,1440]{3,0,2,1:T(4,128)(2,1)S(1)} copy(bf16[4,69,2,1440]{1,2,0,3:T(2,128)(2,1)} %all-to-all-done) | data formatting | bytes 3179520 | tf_op jit(solution)/shard_map/all_to_all | solution.py:150
  208.9 3.8 reshape.78
  212.7 5.6 copy.57
  222.1 61.3 %while.10 = (s32[]{:T(128)}, f32[23,16,3,2,360]{4,1,3,2,0:T(8,128)}, f32[23,16,3,2,360]{4,3,2,0,1:T(2,128)}, f32[23,3]{1,0:T(8,128)S(1)}, s32[]{:T(128)}) while((s32[]{:T(128)}, f32[23,16,3,2,360]{4,1,3,2,0:T(8,128)}, f32[23,16,3,2,360]{4,3,2,0,1:T(2,128)}, f32[23,3]{1,0:T(8,128)S(1)}, s32[]{:T(128)}) %tuple.48), condition=%wide.region_2.3_spmd, body=%wide.region_0.2_spmd.sunk | while | flops 3283202 | bytes 1253493 | solution.py:159
  291.0 25.7 %all_to_all.27 = bf16[16,69,2,360]{3,2,1,0:T(2,128)(2,1)S(1)} all-to-all(bf16[16,69,2,360]{3,2,1,0:T(2,128)(2,1)S(1)} %copy.62), channel_id=1, replica_groups=mesh['mem'=4,'lat'=8] {'mem'}, dimensions={0} | all-to-all | bytes 3179520 | tf_op jit(solution)/shard_map/all_to_all | solution.py:167
  334.7 22.2 %collective-permute-start.4 = (bf16[4,69,1,1440]{3,0,2,1:T(4,128)(2,1)S(1)}, bf16[4,69,1,1440]{3,0,2,1:T(4,128)(2,1)S(1)}, u32[]{:S(2)}, u32[]{:S(2)}) collective-permute-start(bf16[4,69,1,1440]{3,0,2,1:T(4,128)(2,1)S(1)} %copy.65), channel_id=1, source_target_pairs={{0,1},{1,2},{2,3},{3,4},{4,5},{5,6},{6,7},{8,9},{9,10},{10,11},{11... | collective-permute-start | bytes 2384648 | tf_op jit(solution)/shard_map/ppermute | solution.py:15
  364.4 43.1 %collective-permute-done.5 = bf16[4,69,1,1440]{3,0,2,1:T(4,128)(2,1)S(1)} collective-permute-done((bf16[4,69,1,1440]{3,0,2,1:T(4,128)(2,1)S(1)}, bf16[4,69,1,1440]{3,0,2,1:T(4,128)(2,1)S(1)}, u32[]{:S(2)}, u32[]{:S(2)}) %collective-permute-start.5) | collective-permute-done | bytes 794912 | tf_op jit(solution)/shard_map/ppermute | solution.py:17
  407.8 4.2 fusion.98
  412.0 4.2 fusion.95
  416.3 4.1 fusion.104
  420.4 4.1 fusion.108
  424.5 4.2 fusion.101
  428.6 4.0 fusion.57
  436.2 21.4 %fusion.19 = bf16[4,2,1440,128]{3,2,1,0:T(8,128)(2,1)} fusion(f32[4,2,1440,128]{3,2,1,0:T(8,128)} %get-tuple-element.82, f32[4,2,1440,128]{3,2,1,0:T(8,128)} %fusion.61, f32[4,2,1440,128]{3,2,1,0:T(8,128)} %fusion.108, f32[4,2,1440,128]{3,2,1,0:T(8,128)} %fusion.95, f32[4,2,1440,128]{3,2,1,0:T(8,128)} %fusion.216, f32[4,2,1440,128]{3,2,1,0:T(8,128)} %fusion.101, ...), kind=kOutput, calls=%fused_computation.39 | convolution fusion | flops 245007360 | bytes 59526144 | tf_op jit(solution)/shard_map/mvrl,cv->mrlc/dot_general | solution.py:73
  457.6 3.9 fusion.118
  473.5 17.4 %collective-permute-start.6 = (bf16[4,1,1440,128]{3,2,1,0:T(8,128)(2,1)}, bf16[4,1,1440,128]{3,2,1,0:T(8,128)(2,1)}, u32[]{:S(2)}, u32[]{:S(2)}) collective-permute-start(bf16[4,1,1440,128]{3,2,1,0:T(8,128)(2,1)} %get-tuple-element.63), channel_id=1, source_target_pairs={{0,1},{1,2},{2,3},{3,4},{4,5},{5,6},{6,7},{8,9},{9,10},{10,11},{11... | collective-permute-start | bytes 4423688 | tf_op jit(solution)/shard_map/ppermute | solution.py:15
  493.8 5.2 fusion.175
  499.1 122.8 %all-reduce.3.cloned.1.call-done = (f32[3,3,128,128]{3,2,1,0:T(8,128)}, f32[3,3,128,69]{2,3,1,0:T(8,128)}) async-done(((f32[3,3,128,128]{3,2,1,0:T(8,128)}, f32[3,3,128,69]{2,3,1,0:T(8,128)}), (f32[3,3,128,128]{3,2,1,0:T(8,128)}, f32[3,3,128,69]{2,3,1,0:T(8,128)})) %all-reduce.3.cloned.1.call-update) | async-done | bytes 907792 | tf_op jit(solution)/shard_map/psum | solution.py:178
  625.5 7.7 %fusion.4 = (bf16[4,4,1441,128]{3,2,1,0:T(8,128)(2,1)S(1)}, bf16[4,4,1441,128]{3,2,1,0:T(8,128)(2,1)S(1)}) fusion(bf16[4,1,1440,128]{3,2,1,0:T(8,128)(2,1)S(1)} %collective-permute-done.7, bf16[4,2,1440,128]{3,2,1,0:T(8,128)(2,1)} %fusion.19, bf16[4,1,1440,128]{3,2,1,0:T(8,128)(2,1)} %collective-permute-done.6), kind=kLoop, calls=%fused_computation.17 | loop fusion | flops 70828032 | bytes 17702912 | tf_op jit(solution)/shard_map/concatenate | solution.py:26
  633.2 3.9 fusion.45
  651.5 4.8 fusion.24
  659.8 19.4 %add_convert_fusion = bf16[4,2,1440,128]{3,2,1,0:T(8,128)(2,1)} fusion(f32[4,2,1440,128]{3,2,1,0:T(8,128)} %fusion.24, f32[4,2,1440,128]{3,2,1,0:T(8,128)} %fusion.43, f32[4,2,1440,128]{3,2,1,0:T(8,128)} %fusion.45, f32[4,2,1440,128]{3,2,1,0:T(8,128)} %fusion.175, f32[4,2,1440,128]{3,2,1,0:T(8,128)} %fusion.47, f32[4,2,1440,128]{3,2,1,0:T(8,128)} %fusion.49, ...), kind=kOutput, calls=%fused_computation.40 | convolution fusion | flops 390758400 | bytes 53116928 | tf_op jit(solution)/shard_map/mrlo,co->mrlc/dot_general | solution.py:92
  (269 shorter events, 193.1 us)
Async XLA Ops:
  7.2 147.7 %copy-start = (f32[69,2,1440]{2,1,0:T(2,128)S(1)}, f32[69,2,1440]{2,1,0:T(2,128)}, u32[]{:S(2)}) copy-start(f32[69,2,1440]{2,1,0:T(2,128)} %param.11) | copy-start | bytes 2384644
  7.2 6.0 copy-start.9
  7.2 6.0 copy-start.21
  9.4 7.3 %collective-permute-start = (bf16[4,1,1440,128]{3,2,1,0:T(8,128)(2,1)S(1)}, bf16[4,1,1440,128]{3,2,1,0:T(8,128)(2,1)S(1)}, u32[]{:S(2)}, u32[]{:S(2)}) collective-permute-start(bf16[4,1,1440,128]{3,2,1,0:T(8,128)(2,1)S(1)} %get-tuple-element.69), channel_id=1, source_target_pairs={{0,1},{1,2},{2,3},{3,4},{4,5},{5,6},{6,7},{8,9},{9,10},{10,11},{11... | collective-permute-start | bytes 4423688 | tf_op jit(solution)/shard_map/ppermute | solution.py:15
  11.9 7.2 %collective-permute-start.1 = (bf16[4,1,1440,128]{3,2,1,0:T(8,128)(2,1)S(1)}, bf16[4,1,1440,128]{3,2,1,0:T(8,128)(2,1)S(1)}, u32[]{:S(2)}, u32[]{:S(2)}) collective-permute-start(bf16[4,1,1440,128]{3,2,1,0:T(8,128)(2,1)S(1)} %get-tuple-element.70), channel_id=1, source_target_pairs={{1,0},{2,1},{3,2},{4,3},{5,4},{6,5},{7,6},{9,8},{10,9},{11,10},{12... | collective-permute-start | bytes 4423688 | tf_op jit(solution)/shard_map/ppermute | solution.py:17
  19.0 22.4 %copy-start.15 = (bf16[4,3,1440,128]{3,2,1,0:T(8,128)(2,1)}, bf16[4,3,1440,128]{3,2,1,0:T(8,128)(2,1)S(1)}, u32[]{:S(2)}) copy-start(bf16[4,3,1440,128]{3,2,1,0:T(8,128)(2,1)S(1)} %get-tuple-element.66) | copy-start | bytes 13271044
  19.6 14.9 %copy-start.2 = (bf16[4,4,1440,128]{3,2,1,0:T(8,128)(2,1)}, bf16[4,4,1440,128]{3,2,1,0:T(8,128)(2,1)S(1)}, u32[]{:S(2)}) copy-start(bf16[4,4,1440,128]{3,2,1,0:T(8,128)(2,1)S(1)} %get-tuple-element.75) | copy-start | bytes 17694724
  19.6 18.3 %copy-start.13 = (bf16[4,3,1440,128]{3,2,1,0:T(8,128)(2,1)}, bf16[4,3,1440,128]{3,2,1,0:T(8,128)(2,1)S(1)}, u32[]{:S(2)}) copy-start(bf16[4,3,1440,128]{3,2,1,0:T(8,128)(2,1)S(1)} %get-tuple-element.76) | copy-start | bytes 13271044
  66.0 34.1 %copy-start.5 = (bf16[4,2,1440,128]{3,2,1,0:T(8,128)(2,1)S(1)}, bf16[4,2,1440,128]{3,2,1,0:T(8,128)(2,1)}, u32[]{:S(2)}) copy-start(bf16[4,2,1440,128]{3,2,1,0:T(8,128)(2,1)} %get-tuple-element.81) | copy-start | bytes 8847364
  66.0 34.1 %copy-start.22 = (bf16[3,3,128,69]{2,3,1,0:T(8,128)(2,1)S(1)}, bf16[3,3,128,69]{2,3,1,0:T(8,128)(2,1)}, u32[]{:S(2)}) copy-start(bf16[3,3,128,69]{2,3,1,0:T(8,128)(2,1)} %param.10) | copy-start | bytes 476932
  68.1 33.7 %collective-permute-start.2 = (bf16[4,1,1440,128]{3,2,1,0:T(8,128)(2,1)S(1)}, bf16[4,1,1440,128]{3,2,1,0:T(8,128)(2,1)S(1)}, u32[]{:S(2)}, u32[]{:S(2)}) collective-permute-start(bf16[4,1,1440,128]{3,2,1,0:T(8,128)(2,1)S(1)} %get-tuple-element.64), channel_id=1, source_target_pairs={{0,1},{1,2},{2,3},{3,4},{4,5},{5,6},{6,7},{8,9},{9,10},{10,11},{11... | collective-permute-start | bytes 4423688 | tf_op jit(solution)/shard_map/ppermute | solution.py:15
  98.5 5.2 collective-permute-start.3
  101.9 29.5 %copy-start.19 = (bf16[4,1,1440,128]{3,2,1,0:T(8,128)(2,1)}, bf16[4,1,1440,128]{3,2,1,0:T(8,128)(2,1)S(1)}, u32[]{:S(2)}) copy-start(bf16[4,1,1440,128]{3,2,1,0:T(8,128)(2,1)S(1)} %collective-permute-done.2) | copy-start | bytes 4423684
  103.7 25.8 %copy-start.17 = (bf16[4,1,1440,128]{3,2,1,0:T(8,128)(2,1)}, bf16[4,1,1440,128]{3,2,1,0:T(8,128)(2,1)S(1)}, u32[]{:S(2)}) copy-start(bf16[4,1,1440,128]{3,2,1,0:T(8,128)(2,1)S(1)} %collective-permute-done.3) | copy-start | bytes 4423684
  111.0 7.7 %copy-start.12 = (bf16[4,4,1441,128]{3,2,1,0:T(8,128)(2,1)}, bf16[4,4,1441,128]{3,2,1,0:T(8,128)(2,1)S(1)}, u32[]{:S(2)}) copy-start(bf16[4,4,1441,128]{3,2,1,0:T(8,128)(2,1)S(1)} %get-tuple-element.56) | copy-start | bytes 17707012
  111.0 22.2 %copy-start.11 = (bf16[4,4,1441,128]{3,2,1,0:T(8,128)(2,1)}, bf16[4,4,1441,128]{3,2,1,0:T(8,128)(2,1)S(1)}, u32[]{:S(2)}) copy-start(bf16[4,4,1441,128]{3,2,1,0:T(8,128)(2,1)S(1)} %get-tuple-element.57) | copy-start | bytes 17707012
  141.4 13.4 %copy-start.26 = (f32[69]{0:T(128)S(1)}, f32[69]{0:T(128)}, u32[]{:S(2)}) copy-start(f32[69]{0:T(128)} %param.13) | copy-start | bytes 832
  141.4 13.4 %copy-start.27 = (f32[69]{0:T(128)S(1)}, f32[69]{0:T(128)}, u32[]{:S(2)}) copy-start(f32[69]{0:T(128)} %param.12) | copy-start | bytes 832
  149.8 51.3 %all-to-all-start = ((bf16[4,69,2,1440]{1,2,0,3:T(2,128)(2,1)}), bf16[4,69,2,1440]{1,2,0,3:T(2,128)(2,1)}, u32[]{:S(2)}, u32[]{:S(2)}) async-start(bf16[4,69,2,1440]{1,2,0,3:T(2,128)(2,1)} %copy.54), calls=%async_computation | async-start | bytes 5898240 | tf_op jit(solution)/shard_map/all_to_all | solution.py:150
  154.7 467.1 %all-reduce.3.cloned.1.call-start = ((), (), s32[]{:S(2)}) async-start(), calls=%async_computation.2 | async-start | bytes 1843200 | tf_op jit(solution)/shard_map/psum | solution.py:178
  212.7 5.6 copy-start.14
  333.1 25.3 %copy-start.18 = (bf16[4,1,1440,128]{3,2,1,0:T(8,128)(2,1)S(1)}, bf16[4,1,1440,128]{3,2,1,0:T(8,128)(2,1)}, u32[]{:S(2)}) copy-start(bf16[4,1,1440,128]{3,2,1,0:T(8,128)(2,1)} %copy-done.17) | copy-start | bytes 4423684
  334.7 29.3 %collective-permute-start.4 = (bf16[4,69,1,1440]{3,0,2,1:T(4,128)(2,1)S(1)}, bf16[4,69,1,1440]{3,0,2,1:T(4,128)(2,1)S(1)}, u32[]{:S(2)}, u32[]{:S(2)}) collective-permute-start(bf16[4,69,1,1440]{3,0,2,1:T(4,128)(2,1)S(1)} %copy.65), channel_id=1, source_target_pairs={{0,1},{1,2},{2,3},{3,4},{4,5},{5,6},{6,7},{8,9},{9,10},{10,11},{11... | collective-permute-start | bytes 2384648 | tf_op jit(solution)/shard_map/ppermute | solution.py:15
  356.9 50.5 %collective-permute-start.5 = (bf16[4,69,1,1440]{3,0,2,1:T(4,128)(2,1)S(1)}, bf16[4,69,1,1440]{3,0,2,1:T(4,128)(2,1)S(1)}, u32[]{:S(2)}, u32[]{:S(2)}) collective-permute-start(bf16[4,69,1,1440]{3,0,2,1:T(4,128)(2,1)S(1)} %copy.66), channel_id=1, source_target_pairs={{1,0},{2,1},{3,2},{4,3},{5,4},{6,5},{7,6},{9,8},{10,9},{11,10},{12... | collective-permute-start | bytes 2384648 | tf_op jit(solution)/shard_map/ppermute | solution.py:17
  407.6 16.8 %copy-start.7 = (bf16[4,69,4,1440]{3,1,2,0:T(8,128)(2,1)}, bf16[4,69,4,1440]{3,1,2,0:T(8,128)(2,1)S(1)}, u32[]{:S(2)}) copy-start(bf16[4,69,4,1440]{3,1,2,0:T(8,128)(2,1)S(1)} %get-tuple-element.78) | copy-start | bytes 9538564
  457.6 8.6 %slice-start = ((s8[5898240]{0:T(1024)(128)(4,1)}), s8[4194304]{0:T(1024)(128)(4,1)S(1)}, s32[]{:S(2)}) async-start(s8[5898240]{0:T(1024)(128)(4,1)} %bitcast.371), calls=%async_computation.3 | async-start | bytes 8388608
  461.6 4.6 slice-start.1
  469.1 21.9 %slice-start.6 = ((s8[4423680]{0:T(1024)(128)(4,1)}), s8[4194304]{0:T(1024)(128)(4,1)S(1)}, s32[]{:S(2)}) async-start(s8[4423680]{0:T(1024)(128)(4,1)} %bitcast.377), calls=%async_computation.9 | async-start | bytes 8388608
  470.1 20.8 %slice-start.7 = ((s8[4423680]{0:T(1024)(128)(4,1)}), s8[229376]{0:T(1024)(128)(4,1)S(1)}, s32[]{:S(2)}) async-start(s8[4423680]{0:T(1024)(128)(4,1)} %bitcast.377), calls=%async_computation.10 | async-start | bytes 458752
  472.2 153.3 %collective-permute-start.7 = (bf16[4,1,1440,128]{3,2,1,0:T(8,128)(2,1)}, bf16[4,1,1440,128]{3,2,1,0:T(8,128)(2,1)S(1)}, u32[]{:S(2)}, u32[]{:S(2)}) collective-permute-start(bf16[4,1,1440,128]{3,2,1,0:T(8,128)(2,1)} %get-tuple-element.62), channel_id=1, source_target_pairs={{1,0},{2,1},{3,2},{4,3},{5,4},{6,5},{7,6},{9,8},{10,9},{11,10},{12... | collective-permute-start | bytes 4423688 | tf_op jit(solution)/shard_map/ppermute | solution.py:17
  473.5 152.0 %collective-permute-start.6 = (bf16[4,1,1440,128]{3,2,1,0:T(8,128)(2,1)}, bf16[4,1,1440,128]{3,2,1,0:T(8,128)(2,1)}, u32[]{:S(2)}, u32[]{:S(2)}) collective-permute-start(bf16[4,1,1440,128]{3,2,1,0:T(8,128)(2,1)} %get-tuple-element.63), channel_id=1, source_target_pairs={{0,1},{1,2},{2,3},{3,4},{4,5},{5,6},{6,7},{8,9},{9,10},{10,11},{11... | collective-permute-start | bytes 4423688 | tf_op jit(solution)/shard_map/ppermute | solution.py:15
  659.8 19.4 %copy-start.1 = (f32[69,2,1440]{2,1,0:T(2,128)S(1)}, f32[69,2,1440]{2,1,0:T(2,128)}, u32[]{:S(2)}) copy-start(f32[69,2,1440]{2,1,0:T(2,128)} %param.11) | copy-start | bytes 2384644
  (14 other events, 38.6 us)
Sparse Core Ops, SparseCore 0:
  494.0 127.8 all-reduce.2
where the time goes:
time: 697 us; the launch traced here: 686 us
  waiting for transfers between devices  214 us (31%)
  matrix products  210 us (30%)
  local copies, waits for them, and re-layouts  90.5 us (13%)
  starting transfers between devices  82.9 us (12%)
  other arithmetic  47.9 us (7%)
  blocking collectives  25.7 us (4%)
  between operations  14.9 us (2%)
    psum x1, waiting for transfers between devices, shards(): inner_sum, head_sum = lax.psum((inner_grad, head_grad), ('mem', 'lat'))  123 us
    ppermute x4, starting transfers between devices, padded_2(): lax.ppermute(tail, axis, [(i, (i + 1) % count) for i in range(ends)])  72.5 us
    dot_general x9, matrix products, field_back(): jnp.einsum('mvrl,cv->mrlc', padded_grad[:, :, 2 - row_off:2 - row_off + b...  53.3 us
    dot_general x9, matrix products, hidden_back(): jnp.einsum('mrlo,co->mrlc', padded_grad[:, 2 - row_off:2 - row_off + band...  50.8 us
    dot_general x9, matrix products, hidden_conv(): jnp.einsum('mrlc,co->mrlo', padded[:, row_off:row_off + band_rows, col_of...  49.8 us
    all_to_all x1, waiting for transfers between devices, shards(): lax.all_to_all(field, 'mem', split_axis=3, concat_axis=0, tiled=True)  46 us
    ppermute x4, waiting for transfers between devices, padded_2(): lax.ppermute(head, axis, [((i + 1) % count, i) for i in range(ends)])  44.9 us
    dot_general x9, matrix products, field_conv(): jnp.einsum('mrlc,cv->mvrl', padded[:, row_off:row_off + band_rows, col_of...  32.1 us
  transfers between devices with their start and end apart: 10, of which 4 were waited for; matrix products, arithmetic and copies ran while one was open for 4% of the time, Pallas kernels for 0%

commit v1 on v0

--- a/solution.py
+++ b/solution.py
@@ -2,6 +2,18 @@
 import jax.numpy as jnp
 from jax import lax
 from jax.sharding import PartitionSpec as P
+
+
+def split_up(x, dim, size):
+    shape = x.shape
+    parts = x.reshape(*shape[:dim], size, shape[dim] // size, *shape[dim + 1 :])
+    return jnp.moveaxis(parts, dim, 0)
+
+
+def in_order(blocks, dim):
+    dims = list(blocks.shape[1:])
+    dims[dim] *= blocks.shape[0]
+    return jnp.moveaxis(blocks, 0, dim).reshape(dims)
 
 
 def padded_2(cells, sides, width):
@@ -147,7 +159,14 @@
     group = 3
     blocks = variables // group
     inverse_blocks = inverse.reshape(blocks, group)
-    gathered = lax.all_to_all(field, "mem", split_axis=3, concat_axis=0, tiled=True)
+    length, place = (lax.axis_size("mem"), lax.axis_index("mem"))
+    pieces_2 = split_up(field, 3, length)
+    done = [pieces_2[place]]
+    for step in range(1, length):
+        sent = pieces_2[place ^ step]
+        done.append(lax.ppermute(sent, "mem", [(i_2, i_2 ^ step) for i_2 in range(length)]))
+    pieces_2 = jnp.stack(done)[place ^ jnp.arange(length)]
+    gathered = in_order(pieces_2, 0)
     values = gathered.astype(jnp.float32)
     members = values.shape[0]
     piece_cells = values.shape[3]

time: 697 us -> 665 us (0.954)
  waiting for transfers between devices: 214 us -> 169 us
  local copies, waits for them, and re-layouts: 90.5 us -> 76.6 us
  matrix products: 210 us -> 218 us
  other arithmetic: 47.9 us -> 55.1 us
  starting transfers between devices: 82.9 us -> 90 us
    all_to_all x1 -> x0, waiting for transfers between devices: 46 us -> none  [shards(): lax.all_to_all(field, 'mem', split_axis=3, concat_axis=0, tiled=True)]
    ppermute x0 -> x3, waiting for transfers between devices: none -> 14.8 us  [shards(): lax.ppermute(sent, 'mem', [(i_2, i_2 ^ step) for i_2 in range(length)])]
    ppermute x4, waiting for transfers between devices: 44.9 us -> 31.2 us  [padded_2(): lax.ppermute(head, axis, [((i + 1) % count, i) for i in range(ends)])]
    transpose x3 -> x1, local copies, waits for them, and re-layouts: 13.2 us -> 3.07 us  [split_groups(): return jnp.moveaxis(shaped, 1, 0)]
    convert_element_type x1 -> x0, local copies, waits for them, and re-layouts: 8.43 us -> none  [shards(): field = field_conv(hidden_wrap, conv_head, band_rows).astype(jnp.bfloat16)]
    all_to_all x1 -> x0, local copies, waits for them, and re-layouts: 7.72 us -> none  [shards(): lax.all_to_all(field, 'mem', split_axis=3, concat_axis=0, tiled=True)]
    ppermute x4, starting transfers between devices: 72.5 us -> 80 us  [padded_2(): lax.ppermute(tail, axis, [(i, (i + 1) % count) for i in range(ends)])]
  transfers between devices with their start and end apart: 10 -> 12, of which waited for: 4 -> 6; matrix products, arithmetic and copies ran while one was open for 4% -> 4% of each run, Pallas kernels for 0% -> 0%
where the time goes in v1:
time: 665 us; the launch traced here: 654 us
  matrix products  218 us (33%)
  waiting for transfers between devices  169 us (25%)
  starting transfers between devices  90 us (14%)
  local copies, waits for them, and re-layouts  76.6 us (12%)
  other arithmetic  55.1 us (8%)
  blocking collectives  30.4 us (5%)
  between operations  15.2 us (2%)
    psum x1, waiting for transfers between devices, shards(): inner_sum, head_sum = lax.psum((inner_grad, head_grad), ('mem', 'lat'))  122 us
    ppermute x4, starting transfers between devices, padded_2(): lax.ppermute(tail, axis, [(i, (i + 1) % count) for i in range(ends)])  80 us
    dot_general x9, matrix products, field_back(): jnp.einsum('mvrl,cv->mrlc', padded_grad[:, :, 2 - row_off:2 - row_off + b...  53.1 us
    dot_general x9, matrix products, hidden_back(): jnp.einsum('mrlo,co->mrlc', padded_grad[:, 2 - row_off:2 - row_off + band...  50.8 us
    dot_general x9, matrix products, hidden_conv(): jnp.einsum('mrlc,co->mrlo', padded[:, row_off:row_off + band_rows, col_of...  49.8 us
    dot_general x9, matrix products, field_conv(): jnp.einsum('mrlc,cv->mvrl', padded[:, row_off:row_off + band_rows, col_of...  37.3 us
    ppermute x4, waiting for transfers between devices, padded_2(): lax.ppermute(head, axis, [((i + 1) % count, i) for i in range(ends)])  31.2 us
    all_to_all x1, blocking collectives, shards(): lax.all_to_all(gradient, 'mem', split_axis=0, concat_axis=3, tiled=True)  30.4 us
  transfers between devices with their start and end apart: 12, of which 6 were waited for; matrix products, arithmetic and copies ran while one was open for 4% of the time, Pallas kernels for 0%

profile of v1, /device:TPU:0, one launch (start us, length us, event | category | flops | bytes accessed | tf_op | source)
XLA Modules:
  0.0 654.1 jit_solution(11128416126597448563)
XLA Ops:
  19.7 4.1 fusion.183
  23.8 4.0 fusion.173
  44.8 21.2 %multiply_convert_fusion = (bf16[4,2,1440,128]{3,2,1,0:T(8,128)(2,1)}, f32[4,2,1440,128]{3,2,1,0:T(8,128)}) fusion(bf16[3,3,128,128]{3,2,1,0:T(8,128)(2,1)S(1)} %copy-done.16, bf16[4,4,1,128]{3,2,1,0:T(2,128)(2,1)S(1)} %get-tuple-element.54, bf16[4,4,1440,128]{3,2,1,0:T(8,128)(2,1)} %copy-done.2, f32[4,2,1440,128]{3,2,1,0:T(8,128)} %fusion.168, ...), kind=kOutput, calls=%fused_computation.42 | convolution fusion | flops 408453120 | bytes 61972480 | tf_op jit(solution)/shard_map/mrlc,co->mrlo/dot_general | solution.py:57
  66.1 3.7 fusion.275
  69.8 31.7 %collective-permute-start.2 = (bf16[4,1,1440,128]{3,2,1,0:T(8,128)(2,1)}, bf16[4,1,1440,128]{3,2,1,0:T(8,128)(2,1)}, u32[]{:S(2)}, u32[]{:S(2)}) collective-permute-start(bf16[4,1,1440,128]{3,2,1,0:T(8,128)(2,1)} %get-tuple-element.60), channel_id=1, source_target_pairs={{0,1},{1,2},{2,3},{3,4},{4,5},{5,6},{6,7},{8,9},{9,10},{10,11},{11... | collective-permute-start | bytes 4423688 | tf_op jit(solution)/shard_map/ppermute | solution.py:27
  102.9 3.8 fusion.218
  107.1 9.6 %fusion.7 = (bf16[4,4,1441,128]{3,2,1,0:T(8,128)(2,1)S(1)}, bf16[4,4,1441,128]{3,2,1,0:T(8,128)(2,1)S(1)}) fusion(bf16[4,1,1440,128]{3,2,1,0:T(8,128)(2,1)} %collective-permute-done.3, bf16[4,2,1440,128]{3,2,1,0:T(8,128)(2,1)S(1)} %copy-done.5, bf16[4,1,1440,128]{3,2,1,0:T(8,128)(2,1)} %collective-permute-done.2), kind=kLoop, calls=%fused_computation.27 | loop fusion | flops 70828032 | bytes 17702912 | tf_op jit(solution)/shard_map/concatenate | solution.py:38
  116.7 4.1 fusion.76
  120.7 3.7 fusion.84
  141.6 8.5 %fusion.71 = bf16[4,69,2,1440]{3,1,2,0:T(8,128)(2,1)} fusion(bf16[4,4,1441,128]{3,2,1,0:T(8,128)(2,1)S(1)} %get-tuple-element.53, f32[4,2,1440,69]{2,3,1,0:T(8,128)S(1)} %fusion.53, f32[4,2,1440,69]{2,3,1,0:T(8,128)} %fusion.76, f32[4,2,1440,69]{2,3,1,0:T(8,128)} %fusion.80, f32[4,2,1440,69]{2,3,1,0:T(8,128)S(1)} %fusion.218, ...), kind=kOutput, calls=%fused_computation.110 | convolution fusion | flops 210643200 | bytes 31071744 | tf_op jit(solution)/shard_map/mrlc,cv->mvrl/dot_general | solution.py:71
  150.1 4.2 reshape.58
  164.5 7.5 %collective-permute-done.4 = bf16[4,69,2,360]{3,1,2,0:T(8,128)(2,1)S(1)} collective-permute-done((bf16[4,69,2,360]{3,1,2,0:T(8,128)(2,1)}, bf16[4,69,2,360]{3,1,2,0:T(8,128)(2,1)S(1)}, u32[]{:S(2)}, u32[]{:S(2)}) %collective-permute-start.4) | collective-permute-done | bytes 397472 | tf_op jit(solution)/shard_map/ppermute | solution.py:167
  172.0 7.3 %collective-permute-done.5 = bf16[4,69,2,360]{3,1,2,0:T(8,128)(2,1)} collective-permute-done((bf16[4,69,2,360]{3,1,2,0:T(8,128)(2,1)S(1)}, bf16[4,69,2,360]{3,1,2,0:T(8,128)(2,1)}, u32[]{:S(2)}, u32[]{:S(2)}) %collective-permute-start.5) | collective-permute-done | bytes 397472 | tf_op jit(solution)/shard_map/ppermute | solution.py:167
  189.7 61.3 %while.10 = (s32[]{:T(128)}, f32[23,16,3,2,360]{4,1,3,2,0:T(8,128)}, f32[23,16,3,2,360]{4,3,2,0,1:T(2,128)}, f32[23,3]{1,0:T(8,128)S(1)}, s32[]{:T(128)}) while((s32[]{:T(128)}, f32[23,16,3,2,360]{4,1,3,2,0:T(8,128)}, f32[23,16,3,2,360]{4,3,2,0,1:T(2,128)}, f32[23,3]{1,0:T(8,128)S(1)}, s32[]{:T(128)}) %tuple.50), condition=%wide.region_2.3_spmd, body=%wide.region_0.2_spmd.sunk | while | flops 3283202 | bytes 1253493 | solution.py:178
  258.7 30.4 %all_to_all.18 = bf16[16,69,2,360]{3,2,1,0:T(2,128)(2,1)S(1)} all-to-all(bf16[16,69,2,360]{3,2,1,0:T(2,128)(2,1)S(1)} %copy.37), channel_id=1, replica_groups=mesh['mem'=4,'lat'=8] {'mem'}, dimensions={0} | all-to-all | bytes 3179520 | tf_op jit(solution)/shard_map/all_to_all | solution.py:186
  307.6 28.2 %collective-permute-start.7 = (bf16[4,69,1,1440]{3,0,2,1:T(4,128)(2,1)S(1)}, bf16[4,69,1,1440]{3,0,2,1:T(4,128)(2,1)S(1)}, u32[]{:S(2)}, u32[]{:S(2)}) collective-permute-start(bf16[4,69,1,1440]{3,0,2,1:T(4,128)(2,1)S(1)} %copy.40), channel_id=1, source_target_pairs={{0,1},{1,2},{2,3},{3,4},{4,5},{5,6},{6,7},{8,9},{9,10},{10,11},{11... | collective-permute-start | bytes 2384648 | tf_op jit(solution)/shard_map/ppermute | solution.py:27
  344.8 30.8 %collective-permute-done.8 = bf16[4,69,1,1440]{3,0,2,1:T(4,128)(2,1)S(1)} collective-permute-done((bf16[4,69,1,1440]{3,0,2,1:T(4,128)(2,1)S(1)}, bf16[4,69,1,1440]{3,0,2,1:T(4,128)(2,1)S(1)}, u32[]{:S(2)}, u32[]{:S(2)}) %collective-permute-start.8) | collective-permute-done | bytes 794912 | tf_op jit(solution)/shard_map/ppermute | solution.py:29
  376.0 4.2 fusion.98
  380.2 4.3 fusion.95
  384.5 4.1 fusion.104
  388.6 4.1 fusion.108
  392.7 4.2 fusion.101
  396.9 3.7 fusion.57
  404.2 21.4 %fusion.19 = bf16[4,2,1440,128]{3,2,1,0:T(8,128)(2,1)} fusion(f32[4,2,1440,128]{3,2,1,0:T(8,128)} %get-tuple-element.82, f32[4,2,1440,128]{3,2,1,0:T(8,128)} %fusion.61, f32[4,2,1440,128]{3,2,1,0:T(8,128)} %fusion.108, f32[4,2,1440,128]{3,2,1,0:T(8,128)} %fusion.95, f32[4,2,1440,128]{3,2,1,0:T(8,128)} %fusion.216, f32[4,2,1440,128]{3,2,1,0:T(8,128)} %fusion.101, ...), kind=kOutput, calls=%fused_computation.40 | convolution fusion | flops 245007360 | bytes 59526144 | tf_op jit(solution)/shard_map/mvrl,cv->mrlc/dot_general | solution.py:85
  425.6 3.9 fusion.118
  441.5 17.5 %collective-permute-start.9 = (bf16[4,1,1440,128]{3,2,1,0:T(8,128)(2,1)}, bf16[4,1,1440,128]{3,2,1,0:T(8,128)(2,1)}, u32[]{:S(2)}, u32[]{:S(2)}) collective-permute-start(bf16[4,1,1440,128]{3,2,1,0:T(8,128)(2,1)} %get-tuple-element.59), channel_id=1, source_target_pairs={{0,1},{1,2},{2,3},{3,4},{4,5},{5,6},{6,7},{8,9},{9,10},{10,11},{11... | collective-permute-start | bytes 4423688 | tf_op jit(solution)/shard_map/ppermute | solution.py:27
  462.0 5.2 fusion.175
  467.2 122.4 %all-reduce.3.cloned.1.call-done = (f32[3,3,128,128]{3,2,1,0:T(8,128)}, f32[3,3,128,69]{2,3,1,0:T(8,128)}) async-done(((f32[3,3,128,128]{3,2,1,0:T(8,128)}, f32[3,3,128,69]{2,3,1,0:T(8,128)}), (f32[3,3,128,128]{3,2,1,0:T(8,128)}, f32[3,3,128,69]{2,3,1,0:T(8,128)})) %all-reduce.3.cloned.1.call-update) | async-done | bytes 907792 | tf_op jit(solution)/shard_map/psum | solution.py:197
  593.3 7.7 %fusion.4 = (bf16[4,4,1441,128]{3,2,1,0:T(8,128)(2,1)S(1)}, bf16[4,4,1441,128]{3,2,1,0:T(8,128)(2,1)S(1)}) fusion(bf16[4,1,1440,128]{3,2,1,0:T(8,128)(2,1)S(1)} %collective-permute-done.10, bf16[4,2,1440,128]{3,2,1,0:T(8,128)(2,1)} %fusion.19, bf16[4,1,1440,128]{3,2,1,0:T(8,128)(2,1)} %collective-permute-done.9), kind=kLoop, calls=%fused_computation.18 | loop fusion | flops 70828032 | bytes 17702912 | tf_op jit(solution)/shard_map/concatenate | solution.py:38
  601.0 3.9 fusion.45
  619.3 4.8 fusion.24
  627.5 19.4 %add_convert_fusion = bf16[4,2,1440,128]{3,2,1,0:T(8,128)(2,1)} fusion(f32[4,2,1440,128]{3,2,1,0:T(8,128)} %fusion.24, f32[4,2,1440,128]{3,2,1,0:T(8,128)} %fusion.43, f32[4,2,1440,128]{3,2,1,0:T(8,128)} %fusion.45, f32[4,2,1440,128]{3,2,1,0:T(8,128)} %fusion.175, f32[4,2,1440,128]{3,2,1,0:T(8,128)} %fusion.47, f32[4,2,1440,128]{3,2,1,0:T(8,128)} %fusion.49, ...), kind=kOutput, calls=%fused_computation.41 | convolution fusion | flops 390758400 | bytes 53116928 | tf_op jit(solution)/shard_map/mrlo,co->mrlc/dot_general | solution.py:104
  (274 shorter events, 205.0 us)
Async XLA Ops:
  7.2 156.3 %copy-start = (f32[69,2,1440]{2,1,0:T(2,128)S(1)}, f32[69,2,1440]{2,1,0:T(2,128)}, u32[]{:S(2)}) copy-start(f32[69,2,1440]{2,1,0:T(2,128)} %param.11) | copy-start | bytes 2384644
  7.2 6.0 copy-start.16
  7.2 582.4 %all-reduce.3.cloned.1.call-start = ((), (), s32[]{:S(2)}) async-start(), calls=%async_computation.1 | async-start | bytes 1843200 | tf_op jit(solution)/shard_map/psum | solution.py:197
  7.2 6.0 copy-start.9
  9.4 7.3 %collective-permute-start = (bf16[4,1,1440,128]{3,2,1,0:T(8,128)(2,1)S(1)}, bf16[4,1,1440,128]{3,2,1,0:T(8,128)(2,1)S(1)}, u32[]{:S(2)}, u32[]{:S(2)}) collective-permute-start(bf16[4,1,1440,128]{3,2,1,0:T(8,128)(2,1)S(1)} %get-tuple-element.65), channel_id=1, source_target_pairs={{0,1},{1,2},{2,3},{3,4},{4,5},{5,6},{6,7},{8,9},{9,10},{10,11},{11... | collective-permute-start | bytes 4423688 | tf_op jit(solution)/shard_map/ppermute | solution.py:27
  11.9 7.2 %collective-permute-start.1 = (bf16[4,1,1440,128]{3,2,1,0:T(8,128)(2,1)S(1)}, bf16[4,1,1440,128]{3,2,1,0:T(8,128)(2,1)S(1)}, u32[]{:S(2)}, u32[]{:S(2)}) collective-permute-start(bf16[4,1,1440,128]{3,2,1,0:T(8,128)(2,1)S(1)} %get-tuple-element.66), channel_id=1, source_target_pairs={{1,0},{2,1},{3,2},{4,3},{5,4},{6,5},{7,6},{9,8},{10,9},{11,10},{12... | collective-permute-start | bytes 4423688 | tf_op jit(solution)/shard_map/ppermute | solution.py:29
  19.0 22.4 %copy-start.14 = (bf16[4,3,1440,128]{3,2,1,0:T(8,128)(2,1)}, bf16[4,3,1440,128]{3,2,1,0:T(8,128)(2,1)S(1)}, u32[]{:S(2)}) copy-start(bf16[4,3,1440,128]{3,2,1,0:T(8,128)(2,1)S(1)} %get-tuple-element.62) | copy-start | bytes 13271044
  19.7 15.0 %copy-start.2 = (bf16[4,4,1440,128]{3,2,1,0:T(8,128)(2,1)}, bf16[4,4,1440,128]{3,2,1,0:T(8,128)(2,1)S(1)}, u32[]{:S(2)}) copy-start(bf16[4,4,1440,128]{3,2,1,0:T(8,128)(2,1)S(1)} %get-tuple-element.75) | copy-start | bytes 17694724
  19.7 18.4 %copy-start.13 = (bf16[4,3,1440,128]{3,2,1,0:T(8,128)(2,1)}, bf16[4,3,1440,128]{3,2,1,0:T(8,128)(2,1)S(1)}, u32[]{:S(2)}) copy-start(bf16[4,3,1440,128]{3,2,1,0:T(8,128)(2,1)S(1)} %get-tuple-element.76) | copy-start | bytes 13271044
  66.1 36.8 %copy-start.19 = (bf16[3,3,128,69]{2,3,1,0:T(8,128)(2,1)S(1)}, bf16[3,3,128,69]{2,3,1,0:T(8,128)(2,1)}, u32[]{:S(2)}) copy-start(bf16[3,3,128,69]{2,3,1,0:T(8,128)(2,1)} %param.10) | copy-start | bytes 476932
  69.8 36.9 %collective-permute-start.2 = (bf16[4,1,1440,128]{3,2,1,0:T(8,128)(2,1)}, bf16[4,1,1440,128]{3,2,1,0:T(8,128)(2,1)}, u32[]{:S(2)}, u32[]{:S(2)}) collective-permute-start(bf16[4,1,1440,128]{3,2,1,0:T(8,128)(2,1)} %get-tuple-element.60), channel_id=1, source_target_pairs={{0,1},{1,2},{2,3},{3,4},{4,5},{5,6},{6,7},{8,9},{9,10},{10,11},{11... | collective-permute-start | bytes 4423688 | tf_op jit(solution)/shard_map/ppermute | solution.py:27
  101.6 5.5 collective-permute-start.3
  102.9 4.2 copy-start.5
  116.6 7.8 %copy-start.12 = (bf16[4,4,1441,128]{3,2,1,0:T(8,128)(2,1)}, bf16[4,4,1441,128]{3,2,1,0:T(8,128)(2,1)S(1)}, u32[]{:S(2)}) copy-start(bf16[4,4,1441,128]{3,2,1,0:T(8,128)(2,1)S(1)} %get-tuple-element.52) | copy-start | bytes 17707012
  116.6 25.0 %copy-start.11 = (bf16[4,4,1441,128]{3,2,1,0:T(8,128)(2,1)}, bf16[4,4,1441,128]{3,2,1,0:T(8,128)(2,1)S(1)}, u32[]{:S(2)}) copy-start(bf16[4,4,1441,128]{3,2,1,0:T(8,128)(2,1)S(1)} %get-tuple-element.53) | copy-start | bytes 17707012
  154.3 9.0 %copy-start.23 = (f32[69]{0:T(128)S(1)}, f32[69]{0:T(128)}, u32[]{:S(2)}) copy-start(f32[69]{0:T(128)} %param.13) | copy-start | bytes 832
  154.4 9.0 %copy-start.24 = (f32[69]{0:T(128)S(1)}, f32[69]{0:T(128)}, u32[]{:S(2)}) copy-start(f32[69]{0:T(128)} %param.12) | copy-start | bytes 832
  158.9 13.1 %collective-permute-start.4 = (bf16[4,69,2,360]{3,1,2,0:T(8,128)(2,1)}, bf16[4,69,2,360]{3,1,2,0:T(8,128)(2,1)S(1)}, u32[]{:S(2)}, u32[]{:S(2)}) collective-permute-start(bf16[4,69,2,360]{3,1,2,0:T(8,128)(2,1)} %bitcast.377), channel_id=1, source_target_pairs={{0,8},{8,0},{16,24},{24,16},{1,9},{9,1},{17,25},{25,17},{2,10},{10... | collective-permute-start | bytes 1192328 | tf_op jit(solution)/shard_map/ppermute | solution.py:167
  160.5 18.8 %collective-permute-start.5 = (bf16[4,69,2,360]{3,1,2,0:T(8,128)(2,1)S(1)}, bf16[4,69,2,360]{3,1,2,0:T(8,128)(2,1)}, u32[]{:S(2)}, u32[]{:S(2)}) collective-permute-start(bf16[4,69,2,360]{3,1,2,0:T(8,128)(2,1)S(1)} %bitcast.401), channel_id=1, source_target_pairs={{0,16},{8,24},{16,0},{24,8},{1,17},{9,25},{17,1},{25,9},{2,18},{10... | collective-permute-start | bytes 1192328 | tf_op jit(solution)/shard_map/ppermute | solution.py:167
  163.1 16.2 %collective-permute-start.6 = (bf16[4,69,2,360]{3,1,2,0:T(8,128)(2,1)S(1)}, bf16[4,69,2,360]{3,1,2,0:T(8,128)(2,1)}, u32[]{:S(2)}, u32[]{:S(2)}) collective-permute-start(bf16[4,69,2,360]{3,1,2,0:T(8,128)(2,1)S(1)} %bitcast.399), channel_id=1, source_target_pairs={{0,24},{8,16},{16,8},{24,0},{1,25},{9,17},{17,9},{25,1},{2,26},{10... | collective-permute-start | bytes 1192328 | tf_op jit(solution)/shard_map/ppermute | solution.py:167
  298.3 4.3 slice-start.4
  307.6 36.9 %collective-permute-start.7 = (bf16[4,69,1,1440]{3,0,2,1:T(4,128)(2,1)S(1)}, bf16[4,69,1,1440]{3,0,2,1:T(4,128)(2,1)S(1)}, u32[]{:S(2)}, u32[]{:S(2)}) collective-permute-start(bf16[4,69,1,1440]{3,0,2,1:T(4,128)(2,1)S(1)} %copy.40), channel_id=1, source_target_pairs={{0,1},{1,2},{2,3},{3,4},{4,5},{5,6},{6,7},{8,9},{9,10},{10,11},{11... | collective-permute-start | bytes 2384648 | tf_op jit(solution)/shard_map/ppermute | solution.py:27
  335.8 39.9 %collective-permute-start.8 = (bf16[4,69,1,1440]{3,0,2,1:T(4,128)(2,1)S(1)}, bf16[4,69,1,1440]{3,0,2,1:T(4,128)(2,1)S(1)}, u32[]{:S(2)}, u32[]{:S(2)}) collective-permute-start(bf16[4,69,1,1440]{3,0,2,1:T(4,128)(2,1)S(1)} %copy.41), channel_id=1, source_target_pairs={{1,0},{2,1},{3,2},{4,3},{5,4},{6,5},{7,6},{9,8},{10,9},{11,10},{12... | collective-permute-start | bytes 2384648 | tf_op jit(solution)/shard_map/ppermute | solution.py:29
  375.8 16.8 %copy-start.7 = (bf16[4,69,4,1440]{3,1,2,0:T(8,128)(2,1)}, bf16[4,69,4,1440]{3,1,2,0:T(8,128)(2,1)S(1)}, u32[]{:S(2)}) copy-start(bf16[4,69,4,1440]{3,1,2,0:T(8,128)(2,1)S(1)} %get-tuple-element.78) | copy-start | bytes 9538564
  425.6 8.5 %slice-start = ((s8[5898240]{0:T(1024)(128)(4,1)}), s8[4194304]{0:T(1024)(128)(4,1)S(1)}, s32[]{:S(2)}) async-start(s8[5898240]{0:T(1024)(128)(4,1)} %bitcast.385), calls=%async_computation.2 | async-start | bytes 8388608
  429.5 4.6 slice-start.1
  437.0 22.0 %slice-start.6 = ((s8[4423680]{0:T(1024)(128)(4,1)}), s8[4194304]{0:T(1024)(128)(4,1)S(1)}, s32[]{:S(2)}) async-start(s8[4423680]{0:T(1024)(128)(4,1)} %bitcast.391), calls=%async_computation.8 | async-start | bytes 8388608
  438.1 21.0 %slice-start.7 = ((s8[4423680]{0:T(1024)(128)(4,1)}), s8[229376]{0:T(1024)(128)(4,1)S(1)}, s32[]{:S(2)}) async-start(s8[4423680]{0:T(1024)(128)(4,1)} %bitcast.391), calls=%async_computation.9 | async-start | bytes 458752
  440.2 153.1 %collective-permute-start.10 = (bf16[4,1,1440,128]{3,2,1,0:T(8,128)(2,1)}, bf16[4,1,1440,128]{3,2,1,0:T(8,128)(2,1)S(1)}, u32[]{:S(2)}, u32[]{:S(2)}) collective-permute-start(bf16[4,1,1440,128]{3,2,1,0:T(8,128)(2,1)} %get-tuple-element.58), channel_id=1, source_target_pairs={{1,0},{2,1},{3,2},{4,3},{5,4},{6,5},{7,6},{9,8},{10,9},{11,10},{12... | collective-permute-start | bytes 4423688 | tf_op jit(solution)/shard_map/ppermute | solution.py:29
  441.5 151.8 %collective-permute-start.9 = (bf16[4,1,1440,128]{3,2,1,0:T(8,128)(2,1)}, bf16[4,1,1440,128]{3,2,1,0:T(8,128)(2,1)}, u32[]{:S(2)}, u32[]{:S(2)}) collective-permute-start(bf16[4,1,1440,128]{3,2,1,0:T(8,128)(2,1)} %get-tuple-element.59), channel_id=1, source_target_pairs={{0,1},{1,2},{2,3},{3,4},{4,5},{5,6},{6,7},{8,9},{9,10},{10,11},{11... | collective-permute-start | bytes 4423688 | tf_op jit(solution)/shard_map/ppermute | solution.py:27
  601.0 4.3 copy-start.8
  627.5 19.4 %copy-start.1 = (f32[69,2,1440]{2,1,0:T(2,128)S(1)}, f32[69,2,1440]{2,1,0:T(2,128)}, u32[]{:S(2)}) copy-start(f32[69,2,1440]{2,1,0:T(2,128)} %param.11) | copy-start | bytes 2384644
  (13 other events, 33.5 us)
Sparse Core Ops, SparseCore 0:
  462.1 127.5 all-reduce.2
